TPU v7x, 32 devices: a whole 2x2x4 slice. The times are simulated.
32 devices in a mesh: fsdp: 2 (over x), rep: 16 (over z, y, core).
Axes of the slice: x: 2, y: 2, z: 4, core: 2. Of those that a mesh axis runs over, the one named last changes fastest.
Arguments:
- images: bfloat16 [128, 197, 384], P(('fsdp', 'rep')), may hold values from -5 to 5
- cotangent: bfloat16 [128, 197, 384], P(('fsdp', 'rep')), may hold values from -6 to 6
- weights: float32 [1777664], P('fsdp'), may hold values from -3 to 3
- first_moment: float32 [1777664], P(('fsdp', 'rep'))
- second_moment: float32 [1777664], P(('fsdp', 'rep')), as said below
Outputs:
- output: bfloat16 [128, 197, 384], P(('fsdp', 'rep'))
- input_grad: bfloat16 [128, 197, 384], P(('fsdp', 'rep'))
- new_weights: float32 [1777664], P('fsdp')
- gradients: float32 [1777664], P(('fsdp', 'rep'))
- new_first: float32 [1777664], P(('fsdp', 'rep'))
- new_second: float32 [1777664], P(('fsdp', 'rep'))
Inputs may be any that keep to these rules, and one draw needn't show every extreme that they name: second_moment is positive.
All inputs are finite; a program needn't handle non-finite values.
Results may differ from a plain program's by a relative error of at most 0.0095.
The roundings to bfloat16 on the way count: a program that leaves them out, or rounds other values in their place, can miss the bound.
Values may be sent and summed in bfloat16 or wider, within the bound.
A program may use at most 128 MiB of HBM per device.

v0:
```python
import jax
import jax.numpy as jnp
from jax import lax
from jax.sharding import PartitionSpec as P

D = 384
H = 6
FF = 1536
norm_eps = 1e-06
half_root = 0.7071067811865476
inv_root_two_pi = 0.3989422804014327
beta_one = 0.9
beta_two = 0.999
learn_rate = 0.02
decay_rate = 0.05
adam_eps = 1e-08


def product(form, left, right):
    return jnp.einsum(form, left, right, preferred_element_type=jnp.float32)


def layer_norm_forward(values):
    centred = values - jnp.mean(values, -1, keepdims=True)
    variance = jnp.mean(centred * centred, -1, keepdims=True)
    inverse = lax.rsqrt(variance + norm_eps)
    return (centred * inverse, inverse)


def layer_norm_backward(d_scaled, scaled, inverse):
    first_mean = jnp.mean(d_scaled, -1, keepdims=True)
    second_mean = jnp.mean(d_scaled * scaled, -1, keepdims=True)
    return (d_scaled - first_mean - scaled * second_mean) * inverse


def unpack(flat_vec):
    edge_one = 3 * D * D
    edge_two = edge_one + D * D
    edge_three = edge_two + D * FF
    edge_four = edge_three + FF * D
    edge_five = edge_four + 8 * D
    w_qkv = flat_vec[:edge_one].reshape(D, 3 * D)
    w_proj = flat_vec[edge_one:edge_two].reshape(D, D)
    w_fc1 = flat_vec[edge_two:edge_three].reshape(D, FF)
    w_fc2 = flat_vec[edge_three:edge_four].reshape(FF, D)
    vectors = flat_vec[edge_four:edge_five].reshape(8, D)
    b_fc1 = flat_vec[edge_five : edge_five + FF]
    return (w_qkv, w_proj, w_fc1, w_fc2, vectors, b_fc1)


def pack(grads, length):
    pieces = [grad.reshape(-1) for grad in grads]
    used = sum((piece_arr.shape[0] for piece_arr in pieces))
    pieces.append(jnp.zeros((length - used,), jnp.float32))
    return jnp.concatenate(pieces)


def layer_block(images, cotangent, fwd_params, bwd_params):
    w_qkv, w_proj, w_fc1, w_fc2, vectors, b_fc1 = fwd_params
    back_qkv, back_proj, back_fc1, back_fc2, back_vectors, back_b1 = bwd_params
    batch, length, width = images.shape
    head_size = width // H
    token_rows = batch * length
    scale = head_size ** (-0.5)
    vector_float = vectors.astype(jnp.float32)
    backward_vector_slice = back_vectors.astype(jnp.float32)
    input_token_rows = images.astype(jnp.float32).reshape(token_rows, width)
    first_centered_scaled, first_inverse_deviation = layer_norm_forward(input_token_rows)
    first_normed_rows = (first_centered_scaled * vector_float[0] + vector_float[1]).astype(
        jnp.bfloat16
    )
    qkv_rows = jnp.dot(first_normed_rows, w_qkv, preferred_element_type=jnp.float32)
    query = (
        (qkv_rows[:, :width] + vector_float[2])
        .astype(jnp.bfloat16)
        .reshape(batch, length, H, head_size)
    )
    key_arr = (
        qkv_rows[:, width : 2 * width].astype(jnp.bfloat16).reshape(batch, length, H, head_size)
    )
    value = (
        (qkv_rows[:, 2 * width :] + vector_float[3])
        .astype(jnp.bfloat16)
        .reshape(batch, length, H, head_size)
    )
    scores = product("bqhd,bkhd->bhqk", query, key_arr) * scale
    top_score = jnp.max(scores, -1, keepdims=True)
    log_total = top_score + jnp.log(jnp.sum(jnp.exp(scores - top_score), -1, keepdims=True))
    probs_bf = jnp.exp(scores - log_total).astype(jnp.bfloat16)
    mixed = (
        product("bhqk,bkhd->bqhd", probs_bf, value).astype(jnp.bfloat16).reshape(token_rows, width)
    )
    residual_stream = (
        input_token_rows
        + jnp.dot(mixed, w_proj, preferred_element_type=jnp.float32)
        + vector_float[4]
    )
    second_centered_scaled, second_inverse_deviation = layer_norm_forward(residual_stream)
    second_normed_rows = (second_centered_scaled * vector_float[5] + vector_float[6]).astype(
        jnp.bfloat16
    )
    preact = jnp.dot(second_normed_rows, w_fc1, preferred_element_type=jnp.float32) + b_fc1.astype(
        jnp.float32
    )
    normal_cdf = 0.5 * (1.0 + jax.scipy.special.erf(preact * half_root))
    activ = (preact * normal_cdf).astype(jnp.bfloat16)
    result = (
        residual_stream
        + jnp.dot(activ, w_fc2, preferred_element_type=jnp.float32)
        + vector_float[7]
    )
    d_out = cotangent.reshape(token_rows, width)
    output_gradient_float = d_out.astype(jnp.float32)
    grad_fc2 = jnp.dot(activ.T, d_out, preferred_element_type=jnp.float32)
    grad_bias2 = jnp.sum(output_gradient_float, 0)
    d_act = jnp.dot(d_out, back_fc2.T, preferred_element_type=jnp.float32)
    d_pre = d_act * (normal_cdf + preact * jnp.exp(-0.5 * preact * preact) * inv_root_two_pi)
    grad_bias1 = jnp.sum(d_pre, 0)
    d_pre_bf = d_pre.astype(jnp.bfloat16)
    grad_fc1 = jnp.dot(second_normed_rows.T, d_pre_bf, preferred_element_type=jnp.float32)
    second_norm_gradient = jnp.dot(d_pre_bf, back_fc1.T, preferred_element_type=jnp.float32)
    gain2_gradient = jnp.sum(second_norm_gradient * second_centered_scaled, 0)
    grad_shift2 = jnp.sum(second_norm_gradient, 0)
    residual_gradient = output_gradient_float + layer_norm_backward(
        second_norm_gradient * backward_vector_slice[5],
        second_centered_scaled,
        second_inverse_deviation,
    )
    grad_pbias = jnp.sum(residual_gradient, 0)
    d_resid_bf = residual_gradient.astype(jnp.bfloat16)
    grad_proj = jnp.dot(mixed.T, d_resid_bf, preferred_element_type=jnp.float32)
    d_mixed = jnp.dot(d_resid_bf, back_proj.T, preferred_element_type=jnp.float32)
    d_mixed = d_mixed.astype(jnp.bfloat16).reshape(batch, length, H, head_size)
    scores_again = product("bqhd,bkhd->bhqk", query, key_arr) * scale
    probs_full = jnp.exp(scores_again - log_total)
    probs_again = probs_full.astype(jnp.bfloat16)
    d_probs = product("bqhd,bkhd->bhqk", d_mixed, value)
    d_value = product("bhqk,bqhd->bkhd", probs_again, d_mixed).reshape(token_rows, width)
    delta = jnp.sum(probs_full * d_probs, -1, keepdims=True)
    d_scores = (probs_full * (d_probs - delta) * scale).astype(jnp.bfloat16)
    d_query = product("bhqk,bkhd->bqhd", d_scores, key_arr).reshape(token_rows, width)
    d_key = product("bhqk,bqhd->bkhd", d_scores, query).reshape(token_rows, width)
    grad_qbias = jnp.sum(d_query, 0)
    grad_vbias = jnp.sum(d_value, 0)
    d_qkv = jnp.concatenate([d_query, d_key, d_value], 1).astype(jnp.bfloat16)
    grad_qkv = jnp.dot(first_normed_rows.T, d_qkv, preferred_element_type=jnp.float32)
    first_norm_gradient = jnp.dot(d_qkv, back_qkv.T, preferred_element_type=jnp.float32)
    gain1_gradient = jnp.sum(first_norm_gradient * first_centered_scaled, 0)
    grad_shift1 = jnp.sum(first_norm_gradient, 0)
    input_gradient = residual_gradient + layer_norm_backward(
        first_norm_gradient * backward_vector_slice[0],
        first_centered_scaled,
        first_inverse_deviation,
    )
    grad_vectors = jnp.stack(
        [
            gain1_gradient,
            grad_shift1,
            grad_qbias,
            grad_vbias,
            grad_pbias,
            gain2_gradient,
            grad_shift2,
            grad_bias2,
        ]
    )
    grads = (grad_qkv, grad_proj, grad_fc1, grad_fc2, grad_vectors, grad_bias1)
    out_block = result.astype(jnp.bfloat16).reshape(batch, length, width)
    input_block = input_gradient.astype(jnp.bfloat16).reshape(batch, length, width)
    return (out_block, input_block, grads)


def adamw(weight_vals, grad_vals, first_vals, second_vals):
    first_new = beta_one * first_vals + (1.0 - beta_one) * grad_vals
    second_new = beta_two * second_vals + (1.0 - beta_two) * grad_vals * grad_vals
    first_hat = first_new / (1.0 - beta_one**2)
    second_hat = second_new / (1.0 - beta_two**2)
    updated = weight_vals - learn_rate * (
        first_hat / (jnp.sqrt(second_hat) + adam_eps) + decay_rate * weight_vals
    )
    return (updated, first_new, second_new)


def on_device(images, cotangent, weights, first_moment, second_moment):
    half_bf = weights.astype(jnp.bfloat16)
    params = unpack(lax.all_gather(half_bf, "fsdp", axis=0, tiled=True))
    back_params = unpack(lax.all_gather(half_bf, "fsdp", axis=0, tiled=True))
    output, input_grad, grads = layer_block(images, cotangent, params, back_params)
    flat_grad = pack(grads, 2 * weights.shape[0])
    half_grad = lax.psum_scatter(
        flat_grad.astype(jnp.bfloat16), "fsdp", scatter_dimension=0, tiled=True
    ).astype(jnp.float32)
    piece_len = first_moment.shape[0]
    offset = lax.axis_index("rep") * piece_len
    summed_all = lax.psum(half_grad, "rep")
    own_grad = lax.dynamic_slice_in_dim(summed_all, offset, piece_len)
    own_weights = lax.dynamic_slice_in_dim(weights, offset, piece_len)
    new_own, new_first, new_second = adamw(own_weights, own_grad, first_moment, second_moment)
    new_weights = lax.all_gather(new_own, "rep", axis=0, tiled=True)
    return (output, input_grad, new_weights, own_grad, new_first, new_second)


def solution(mesh):
    in_specs = (
        P(("fsdp", "rep"), None, None),
        P(("fsdp", "rep"), None, None),
        P("fsdp"),
        P(("fsdp", "rep")),
        P(("fsdp", "rep")),
    )
    out_specs = (
        P(("fsdp", "rep"), None, None),
        P(("fsdp", "rep"), None, None),
        P("fsdp"),
        P(("fsdp", "rep")),
        P(("fsdp", "rep")),
        P(("fsdp", "rep")),
    )
    return jax.shard_map(
        on_device, mesh=mesh, in_specs=in_specs, out_specs=out_specs, check_vma=False
    )
```

profile of v0, /device:TPU:0, one launch (start us, length us, event | category | flops | bytes accessed | tf_op | source)
XLA Modules:
  0.0 480.9 jit_solution(8858606511135499291)
XLA Ops:
  7.2 3.4 convert_element_type.75
  12.6 1.1 copy.81
  17.3 1.4 reshape.202
  18.8 44.2 %all-gather.4.cloned.1.call-done = bf16[1777664]{0:T(1024)(128)(2,1)} async-done(((bf16[888832]{0:T(1024)(128)(2,1)}), bf16[1777664]{0:T(1024)(128)(2,1)}) %all-gather.4.cloned.1.call-update) | async-done | bytes 3555344 | tf_op jit(solution)/shard_map/all_gather | solution.py:186
  66.9 1.2 convert_element_type.78
  68.2 1.9 reshape.203
  70.1 2.8 fusion.60
  72.9 3.4 reshape.210
  76.4 2.2 reshape.209
  78.6 2.4 fusion.66
  82.1 2.0 reshape.227
  84.1 1.9 copy.90
  86.0 3.3 reshape.228
  89.2 2.7 copy.91
  91.9 2.0 reshape.226
  93.9 1.9 copy.92
  95.8 2.0 multiply_reduce_fusion.1
  98.8 1.2 copy-done
  100.0 1.1 fusion.30
  101.1 1.5 copy.94
  102.6 2.7 reshape.207
  105.3 2.0 fusion.62
  107.7 4.7 multiply_convert_fusion.1
  112.4 16.3 %fusion.65 = (bf16[1536]{0:T(1024)(128)(2,1)}, bf16[788,1536]{1,0:T(8,128)(2,1)S(1)}) fusion(f32[788,1536]{1,0:T(8,128)S(1)} %get-tuple-element.61, f32[1536]{0:T(1024)S(1)} %slice_convert_fusion.2, bf16[788,384]{1,0:T(8,128)(2,1)S(1)} %copy-done.13, bf16[1536,384]{1,0:T(8,128)(2,1)S(1)} %copy-done.18), kind=kOutput, calls=%fused_computation.106 | convolution fusion | flops 944085504 | bytes 9056256 | tf_op jit(solution)/shard_map/dot_general | solution.py:116
  128.8 2.2 multiply_reduce_fusion.2
  131.0 2.6 convolution_convert_fusion.1
  134.7 1.2 convolution_convert_fusion.5
  136.0 1.4 convolution_convert_fusion.4
  137.4 3.0 reshape.229
  140.4 2.6 copy.97
  143.1 5.1 %bitcast_convert_fusion = (bf16[4,197,6,64]{1,3,2,0:T(8,128)(2,1)}, f32[4,6,64,197]{3,2,1,0:T(8,128)}) fusion(bf16[4,197,6,64]{1,3,2,0:T(8,128)(2,1)} %copy.97, f32[4,6,197,197]{2,3,1,0:T(8,128)} %copy-done, f32[4,6,197]{2,1,0:T(8,128)S(1)} %log_add_fusion), kind=kOutput, calls=%fused_computation.27 | convolution fusion | flops 122318088 | bytes 6165312 | tf_op jit(solution)/shard_map/bhqk,bqhd->bkhd/dot_general | solution.py:20
  148.2 3.1 fusion.67
  151.3 10.3 %fusion.31 = bf16[4,197,6,64]{1,3,2,0:T(8,128)(2,1)} fusion(bf16[4,197,6,64]{1,3,2,0:T(8,128)(2,1)} %copy-done.11, f32[4,6,197,197]{2,3,1,0:T(8,128)} %fusion.67, f32[4,6,197,197]{2,3,1,0:T(8,128)} %copy-done, f32[4,6,197]{2,1,0:T(8,128)S(1)} %log_add_fusion), kind=kOutput, calls=%fused_computation.39 | convolution fusion | flops 127911504 | bytes 8680608 | tf_op jit(solution)/shard_map/bhqk,bqhd->bkhd/dot_general | solution.py:20
  161.6 10.5 %bitcast_convert_fusion.1 = (bf16[4,197,6,64]{1,3,2,0:T(8,128)(2,1)}, f32[4,6,64,197]{3,2,1,0:T(8,128)}) fusion(bf16[4,197,6,64]{1,3,2,0:T(8,128)(2,1)S(1)} %copy-done.12, f32[4,6,197,197]{2,3,1,0:T(8,128)} %fusion.67, f32[4,6,197,197]{2,3,1,0:T(8,128)} %copy-done, f32[4,6,197]{2,1,0:T(8,128)S(1)} %log_add_fusion), kind=kOutput, calls=%fused_computation.29 | convolution fusion | flops 127911504 | bytes 9890976 | tf_op jit(solution)/shard_map/bhqk,bkhd->bqhd/dot_general | solution.py:20
  172.1 1.7 copy.107
  173.9 1.4 reshape.216
  175.3 1.7 copy.101
  177.1 1.5 reshape.214
  178.5 1.7 copy.104
  180.3 1.4 reshape.215
  181.7 1.3 constant_dynamic-update-slice_fusion.2
  183.0 1.2 constant_dynamic-update-slice_fusion.1
  184.2 1.2 constant_dynamic-update-slice_fusion
  185.5 2.8 multiply_reduce_fusion.3
  188.3 2.6 convolution_convert_fusion.2
  190.9 2.8 convolution_convert_fusion
  193.8 3.1 reshape.221
  196.9 3.5 reshape.220
  201.2 1.6 bitcast_reduce_fusion
  202.9 1.6 bitcast_reduce_fusion.1
  204.6 2.1 reshape.218
  207.7 1.7 constant_dynamic-update-slice_fusion.7
  209.4 1.1 constant_dynamic-update-slice_fusion.6
  210.5 1.1 constant_dynamic-update-slice_fusion.5
  212.2 1.4 dynamic-update-slice.5
  213.7 1.4 dynamic-update-slice.6
  216.4 93.6 %all-reduce.6.cloned.1.call-done = bf16[1777664]{0:T(1024)(128)(2,1)} async-done(((bf16[1777664]{0:T(1024)(128)(2,1)}), bf16[1777664]{0:T(1024)(128)(2,1)}) %all-reduce.6.cloned.1.call-update) | async-done | bytes 3555344
  310.0 3.5 dynamic-slice_convert_fusion
  313.6 107.2 %all-reduce.4.cloned.1.call-done = f32[888832]{0:T(1024)} async-done(((f32[888832]{0:T(1024)}), f32[888832]{0:T(1024)}) %all-reduce.4.cloned.1.call-update) | async-done | bytes 3555344 | tf_op jit(solution)/shard_map/psum | solution.py:195
  420.8 2.1 multiply_subtract_fusion
  423.7 4.3 fusion.29
  428.0 1.3 reshape.211
  432.6 37.5 %all-gather.6.cloned.1.call-done = f32[16,1,55552]{2,1,0:T(1,128)} async-done(((f32[1,1,55552]{2,1,0:T(1,128)}), f32[16,1,55552]{2,1,0:T(1,128)}) %all-gather.6.cloned.1.call-update) | async-done | bytes 3555344 | tf_op jit(solution)/shard_map/all_gather | solution.py:199
  470.1 4.0 copy.135
  (128 shorter events, 20.6 us)
Async XLA Ops:
  7.2 55.9 %all-gather.4.cloned.1.call-start = ((), (), s32[]{:S(2)}) async-start(), calls=%async_computation | async-start | bytes 5332992 | tf_op jit(solution)/shard_map/all_gather | solution.py:186
  10.6 1.1 copy-start.15
  10.6 2.0 copy-start.4
  10.6 299.4 %all-reduce.6.cloned.1.call-start = ((), (), s32[]{:S(2)}) async-start(), calls=%async_computation.3 | async-start | bytes 7110656
  18.8 86.6 %copy-start.1 = (f32[788,384]{1,0:T(8,128)}, f32[788,384]{1,0:T(8,128)S(1)}, u32[]{:S(2)}) copy-start(f32[788,384]{1,0:T(8,128)S(1)} %reshape.202) | copy-start | bytes 3631108
  64.3 3.9 copy-start.22
  64.3 3.9 copy-start.26
  66.0 2.2 slice-start
  86.0 9.9 %copy-start.11 = (bf16[4,197,6,64]{1,3,2,0:T(8,128)(2,1)}, bf16[4,197,6,64]{1,3,2,0:T(8,128)(2,1)S(1)}, u32[]{:S(2)}) copy-start(bf16[4,197,6,64]{1,3,2,0:T(8,128)(2,1)S(1)} %copy.90) | copy-start | bytes 1815556
  97.8 2.2 copy-start
  105.3 2.3 copy-start.9
  107.7 4.7 copy-start.13
  107.7 4.7 copy-start.18
  112.4 16.3 %copy-start.19 = (bf16[384,1536]{1,0:T(8,128)(2,1)S(1)}, bf16[384,1536]{1,0:T(8,128)(2,1)}, u32[]{:S(2)}) copy-start(bf16[384,1536]{1,0:T(8,128)(2,1)} %reshape.209) | copy-start | bytes 3538948
  133.6 1.1 copy-start.6
  143.1 5.1 %copy-start.5 = (bf16[4,197,6,64]{1,3,2,0:T(8,128)(2,1)S(1)}, bf16[4,197,6,64]{1,3,2,0:T(8,128)(2,1)}, u32[]{:S(2)}) copy-start(bf16[4,197,6,64]{1,3,2,0:T(8,128)(2,1)} %copy.97) | copy-start | bytes 1815556
  151.3 10.3 %copy-start.12 = (bf16[4,197,6,64]{1,3,2,0:T(8,128)(2,1)S(1)}, bf16[4,197,6,64]{1,3,2,0:T(8,128)(2,1)}, u32[]{:S(2)}) copy-start(bf16[4,197,6,64]{1,3,2,0:T(8,128)(2,1)} %copy.91) | copy-start | bytes 1815556
  181.7 3.7 copy-start.2
  181.7 3.7 copy-start.10
  181.7 3.7 copy-start.23
  181.7 3.7 copy-start.24
  181.7 3.7 copy-start.25
  185.5 2.8 copy-start.27
  188.3 2.6 copy-start.14
  188.3 2.6 copy-start.34
  193.8 6.6 %copy-start.32 = (bf16[384]{0:T(512)(128)(2,1)S(1)}, bf16[384]{0:T(512)(128)(2,1)}, u32[]{:S(2)}) copy-start(bf16[384]{0:T(512)(128)(2,1)} %get-tuple-element.30) | copy-start | bytes 2308
  193.8 6.6 %copy-start.31 = (bf16[384]{0:T(512)(128)(2,1)S(1)}, bf16[384]{0:T(512)(128)(2,1)}, u32[]{:S(2)}) copy-start(bf16[384]{0:T(512)(128)(2,1)} %get-tuple-element.36) | copy-start | bytes 2308
  193.8 6.6 %copy-start.17 = (bf16[384,384]{1,0:T(8,128)(2,1)S(1)}, bf16[384,384]{1,0:T(8,128)(2,1)}, u32[]{:S(2)}) copy-start(bf16[384,384]{1,0:T(8,128)(2,1)} %convolution_convert_fusion.5) | copy-start | bytes 884740
  202.8 3.8 copy-start.28
  206.7 2.7 copy-start.8
  206.7 3.8 copy-start.7
  209.4 2.8 copy-start.29
  211.6 3.5 copy-start.33
  215.1 205.7 %all-reduce.4.cloned.1.call-start = ((), (), s32[]{:S(2)}) async-start(), calls=%async_computation.1 | async-start | bytes 7110656 | tf_op jit(solution)/shard_map/psum | solution.py:195
  313.5 107.3 %copy-start.20 = (f32[55552]{0:T(1024)S(1)}, f32[55552]{0:T(1024)}, u32[]{:S(2)}) copy-start(f32[55552]{0:T(1024)} %param.8) | copy-start | bytes 666628
  313.5 107.3 %copy-start.21 = (f32[55552]{0:T(1024)S(1)}, f32[55552]{0:T(1024)}, u32[]{:S(2)}) copy-start(f32[55552]{0:T(1024)} %param.9) | copy-start | bytes 666628
  313.5 110.2 %copy-start.30 = (f32[384]{0:T(512)S(1)}, f32[384]{0:T(512)}, u32[]{:S(2)}) copy-start(f32[384]{0:T(512)} %get-tuple-element.48) | copy-start | bytes 4612
  313.5 156.6 %all-gather.6.cloned.1.call-start = ((), (), s32[]{:S(2)}) async-start(), calls=%async_computation.2 | async-start | bytes 3777536 | tf_op jit(solution)/shard_map/all_gather | solution.py:199
  428.0 2.4 copy-start.3
  429.3 1.6 copy-start.16
Sparse Core Ops, SparseCore 0:
  10.8 52.2 all-gather.3
  215.2 94.7 all-reduce.5
  314.2 106.4 all-reduce.3
  423.8 46.2 all-gather.5
where the time goes:
time: 486 us; the launch traced here: 481 us
  waiting for transfers between devices  283 us (58%)
  local copies, waits for them, and re-layouts  88.2 us (18%)
  matrix products  77.6 us (16%)
  other arithmetic  17.2 us (4%)
  between operations  15.1 us (3%)
    psum x1, waiting for transfers between devices, on_device(): summed_all = lax.psum(half_grad, 'rep')  107 us
    unnamed x5, waiting for transfers between devices  93.7 us
    all_gather x1, waiting for transfers between devices, on_device(): params = unpack(lax.all_gather(half_bf, 'fsdp', axis=0, tiled=True))  44.2 us
    all_gather x1, waiting for transfers between devices, on_device(): new_weights = lax.all_gather(new_own, 'rep', axis=0, tiled=True)  37.5 us
    dot_general x6, matrix products, product(): return jnp.einsum(form, left, right, preferred_element_type=jnp.float32)  32.1 us
    unnamed x86, local copies, waits for them, and re-layouts  20.6 us
    dot_general x1, matrix products, layer_block(): d_act = jnp.dot(d_out, back_fc2.T, preferred_element_type=jnp.float32)  16.3 us
  transfers between devices with their start and end apart: 4, of which 4 were waited for; matrix products, arithmetic and copies ran while one was open for 3% of the time, Pallas kernels for 0%

commit v1 on v0

--- a/solution.py
+++ b/solution.py
@@ -14,6 +14,17 @@
 learn_rate = 0.02
 decay_rate = 0.05
 adam_eps = 1e-08
+
+
+def ring_gather(shard, axis, dim):
+    ways = lax.axis_size(axis)
+    pieces = [shard]
+    for far in range(1, ways):
+        pieces.append(
+            lax.ppermute(pieces[far - 1], axis, [(d, (d - 1) % ways) for d in range(ways)])
+        )
+    line = jnp.concatenate(pieces, axis=dim)
+    return jnp.roll(line, lax.axis_index(axis) * shard.shape[dim], axis=dim)
 
 
 def product(form, left, right):
@@ -196,7 +207,7 @@
     own_grad = lax.dynamic_slice_in_dim(summed_all, offset, piece_len)
     own_weights = lax.dynamic_slice_in_dim(weights, offset, piece_len)
     new_own, new_first, new_second = adamw(own_weights, own_grad, first_moment, second_moment)
-    new_weights = lax.all_gather(new_own, "rep", axis=0, tiled=True)
+    new_weights = ring_gather(new_own, "rep", 0)
     return (output, input_grad, new_weights, own_grad, new_first, new_second)
 
 

time: 486 us -> 585 us (1.20)
  starting transfers between devices: 0.16 us -> 62.4 us
  local copies, waits for them, and re-layouts: 88.2 us -> 141 us
  waiting for transfers between devices: 283 us -> 269 us
  matrix products: 77.6 us -> 70.2 us
    ppermute x0 -> x15, starting transfers between devices: none -> 62.3 us  [ring_gather(): lax.ppermute(pieces[far - 1], axis, [(d, (d - 1) % ways) for d in range(w...]
    unnamed x86 -> x128, local copies, waits for them, and re-layouts: 20.6 us -> 65.1 us
    all_gather x1 -> x0, waiting for transfers between devices: 37.5 us -> none  [on_device(): new_weights = lax.all_gather(new_own, 'rep', axis=0, tiled=True)]
    ppermute x0 -> x15, waiting for transfers between devices: none -> 22.8 us  [ring_gather(): lax.ppermute(pieces[far - 1], axis, [(d, (d - 1) % ways) for d in range(w...]
    dot_general x1, matrix products: 16.3 us -> 4.45 us  [layer_block(): d_act = jnp.dot(d_out, back_fc2.T, preferred_element_type=jnp.float32)]
    unnamed x5 -> x4, waiting for transfers between devices: 93.7 us -> 93.6 us
  transfers between devices with their start and end apart: 4 -> 18, of which waited for: 4 -> 15; matrix products, arithmetic and copies ran while one was open for 3% -> 7% of each run, Pallas kernels for 0% -> 0%
where the time goes in v1:
time: 585 us; the launch traced here: 578 us
  waiting for transfers between devices  269 us (46%)
  local copies, waits for them, and re-layouts  141 us (24%)
  matrix products  70.2 us (12%)
  starting transfers between devices  62.4 us (11%)
  other arithmetic  20.5 us (4%)
  between operations  15.1 us (3%)
    psum x1, waiting for transfers between devices, on_device(): summed_all = lax.psum(half_grad, 'rep')  107 us
    unnamed x4, waiting for transfers between devices  93.6 us
    unnamed x128, local copies, waits for them, and re-layouts  65.1 us
    ppermute x15, starting transfers between devices, ring_gather(): lax.ppermute(pieces[far - 1], axis, [(d, (d - 1) % ways) for d in range(w...  62.3 us
    all_gather x1, waiting for transfers between devices, on_device(): params = unpack(lax.all_gather(half_bf, 'fsdp', axis=0, tiled=True))  45 us
    dot_general x6, matrix products, product(): return jnp.einsum(form, left, right, preferred_element_type=jnp.float32)  33.2 us
    ppermute x15, waiting for transfers between devices, ring_gather(): lax.ppermute(pieces[far - 1], axis, [(d, (d - 1) % ways) for d in range(w...  22.8 us
  transfers between devices with their start and end apart: 18, of which 15 were waited for; matrix products, arithmetic and copies ran while one was open for 7% of the time, Pallas kernels for 0%

profile of v1, /device:TPU:0, one launch (start us, length us, event | category | flops | bytes accessed | tf_op | source)
XLA Modules:
  0.0 577.5 jit_solution(16406666578554254514)
XLA Ops:
  7.2 3.4 convert_element_type.75
  18.1 45.0 %all-gather.2.cloned.1.call-done = bf16[1777664]{0:T(1024)(128)(2,1)} async-done(((bf16[888832]{0:T(1024)(128)(2,1)}), bf16[1777664]{0:T(1024)(128)(2,1)}) %all-gather.2.cloned.1.call-update) | async-done | bytes 3555344 | tf_op jit(solution)/shard_map/all_gather | solution.py:197
  67.2 1.9 reshape.203
  69.2 2.4 fusion.66
  72.6 2.0 reshape.224
  74.7 2.0 copy.92
  76.7 2.0 reshape.225
  78.7 1.9 copy.90
  80.7 3.3 reshape.226
  83.9 2.6 copy.91
  86.5 2.0 multiply_reduce_fusion.1
  93.6 2.8 fusion.60
  96.5 2.2 reshape.209
  100.8 2.3 reshape.210
  103.8 4.6 multiply_convert_fusion.1
  108.5 4.4 fusion.65
  112.9 2.2 multiply_reduce_fusion.2
  117.7 3.0 reshape.227
  120.7 2.7 copy.97
  123.4 4.2 fusion.67
  127.6 10.7 %bitcast_convert_fusion.1 = (bf16[4,197,6,64]{1,3,2,0:T(8,128)(2,1)}, f32[4,6,64,197]{3,2,1,0:T(8,128)}) fusion(bf16[4,197,6,64]{1,3,2,0:T(8,128)(2,1)} %copy.91, f32[4,6,197,197]{2,3,1,0:T(8,128)} %fusion.67, f32[4,6,197,197]{2,3,1,0:T(8,128)} %copy-done, f32[4,6,197]{2,1,0:T(8,128)S(1)} %log_add_fusion), kind=kOutput, calls=%fused_computation.29 | convolution fusion | flops 127911504 | bytes 9890976 | tf_op jit(solution)/shard_map/bhqk,bkhd->bqhd/dot_general | solution.py:31
  138.3 10.2 %fusion.31 = bf16[4,197,6,64]{1,3,2,0:T(8,128)(2,1)} fusion(bf16[4,197,6,64]{1,3,2,0:T(8,128)(2,1)} %copy-done.8, f32[4,6,197,197]{2,3,1,0:T(8,128)} %fusion.67, f32[4,6,197,197]{2,3,1,0:T(8,128)} %copy-done, f32[4,6,197]{2,1,0:T(8,128)S(1)} %log_add_fusion), kind=kOutput, calls=%fused_computation.39 | convolution fusion | flops 127911504 | bytes 8680608 | tf_op jit(solution)/shard_map/bhqk,bqhd->bkhd/dot_general | solution.py:31
  148.5 5.0 bitcast_convert_fusion
  155.6 2.0 constant_dynamic-update-slice_fusion.2
  157.6 2.6 copy.104
  160.2 3.1 reshape.215
  163.3 2.6 copy.107
  166.0 2.7 reshape.216
  168.7 2.0 constant_dynamic-update-slice_fusion.1
  170.7 2.0 constant_dynamic-update-slice_fusion
  172.8 4.8 multiply_reduce_fusion.3
  177.6 2.6 convolution_convert_fusion.2
  181.5 2.6 convolution_convert_fusion.1
  184.1 2.0 reshape.218
  188.2 3.5 reshape.220
  191.7 4.6 convolution_convert_fusion
  196.3 3.2 reshape.221
  203.8 2.4 constant_dynamic-update-slice_fusion.7
  212.0 93.6 %all-reduce.6.cloned.1.call-done = bf16[1777664]{0:T(1024)(128)(2,1)} async-done(((bf16[1777664]{0:T(1024)(128)(2,1)}), bf16[1777664]{0:T(1024)(128)(2,1)}) %all-reduce.6.cloned.1.call-update) | async-done | bytes 3555344
  305.6 3.5 dynamic-slice_convert_fusion
  309.1 107.2 %all-reduce.4.cloned.1.call-done = f32[888832]{0:T(1024)} async-done(((f32[888832]{0:T(1024)}), f32[888832]{0:T(1024)}) %all-reduce.4.cloned.1.call-update) | async-done | bytes 3555344 | tf_op jit(solution)/shard_map/psum | solution.py:206
  416.3 2.2 constant_dynamic-update-slice_fusion.4
  419.1 3.5 collective-permute-done
  422.6 4.6 collective-permute-start.1
  427.2 3.5 collective-permute-done.1
  430.7 4.6 collective-permute-start.2
  435.4 3.5 collective-permute-done.2
  438.8 4.6 collective-permute-start.3
  443.5 3.5 collective-permute-done.3
  446.9 4.7 collective-permute-start.4
  451.7 4.3 fusion.29
  460.1 3.8 collective-permute-done.5
  463.9 4.5 collective-permute-start.6
  468.4 3.5 collective-permute-done.6
  471.9 4.7 collective-permute-start.7
  476.6 2.2 add_convert_fusion.1
  480.4 4.6 collective-permute-start.8
  488.8 4.5 collective-permute-start.9
  496.8 4.6 collective-permute-start.10
  504.9 4.6 collective-permute-start.11
  513.0 4.6 collective-permute-start.12
  521.1 4.6 collective-permute-start.13
  529.2 4.6 collective-permute-start.14
  566.0 4.8 dynamic_slice.12
  (201 shorter events, 97.6 us)
Async XLA Ops:
  7.2 3.6 copy-start.3
  7.2 55.9 %all-gather.2.cloned.1.call-start = ((), (), s32[]{:S(2)}) async-start(), calls=%async_computation | async-start | bytes 5332992 | tf_op jit(solution)/shard_map/all_gather | solution.py:197
  10.7 2.7 copy-start.13
  10.7 294.9 %all-reduce.6.cloned.1.call-start = ((), (), s32[]{:S(2)}) async-start(), calls=%async_computation.2 | async-start | bytes 7110656
  13.3 85.3 %copy-start.1 = (f32[788,384]{1,0:T(8,128)}, f32[788,384]{1,0:T(8,128)S(1)}, u32[]{:S(2)}) copy-start(f32[788,384]{1,0:T(8,128)S(1)} %reshape.202) | copy-start | bytes 3631108
  63.1 4.1 slice-start
  64.5 0.6 copy-start.33
  64.5 4.7 copy-start.29
  80.6 7.9 %copy-start.8 = (bf16[4,197,6,64]{1,3,2,0:T(8,128)(2,1)}, bf16[4,197,6,64]{1,3,2,0:T(8,128)(2,1)S(1)}, u32[]{:S(2)}) copy-start(bf16[4,197,6,64]{1,3,2,0:T(8,128)(2,1)S(1)} %copy.90) | copy-start | bytes 1815556
  88.6 2.2 copy-start
  89.5 3.3 slice-start.1
  93.6 5.0 copy-start.9
  103.1 5.3 copy-start.14
  103.8 4.6 copy-start.12
  108.4 4.5 copy-start.15
  108.4 4.5 copy-start.26
  112.9 2.2 copy-start.10
  138.3 10.3 %copy-start.4 = (bf16[4,197,6,64]{1,3,2,0:T(8,128)(2,1)S(1)}, bf16[4,197,6,64]{1,3,2,0:T(8,128)(2,1)}, u32[]{:S(2)}) copy-start(bf16[4,197,6,64]{1,3,2,0:T(8,128)(2,1)} %copy.97) | copy-start | bytes 1815556
  148.5 5.0 copy-start.22
  160.2 12.5 %copy-start.7 = (bf16[384,1152]{1,0:T(8,128)(2,1)S(1)}, bf16[384,1152]{1,0:T(8,128)(2,1)}, u32[]{:S(2)}) copy-start(bf16[384,1152]{1,0:T(8,128)(2,1)} %reshape.203) | copy-start | bytes 2654212
  160.2 12.5 %copy-start.30 = (f32[384]{0:T(512)S(1)}, f32[384]{0:T(512)}, u32[]{:S(2)}) copy-start(f32[384]{0:T(512)} %copy-done.29) | copy-start | bytes 4612
  160.2 12.5 %copy-start.31 = (f32[788]{0:T(1024)S(1)}, f32[788]{0:T(1024)}, u32[]{:S(2)}) copy-start(f32[788]{0:T(1024)} %rsqrt.22) | copy-start | bytes 9460
  160.2 12.5 %copy-start.32 = (f32[788]{0:T(1024)S(1)}, f32[788]{0:T(1024)}, u32[]{:S(2)}) copy-start(f32[788]{0:T(1024)} %div.48) | copy-start | bytes 9460
  172.7 4.8 copy-start.2
  172.8 4.8 copy-start.23
  172.8 4.8 copy-start.34
  177.5 2.7 copy-start.5
  177.6 3.9 copy-start.11
  177.6 3.9 copy-start.27
  177.6 3.9 copy-start.28
  196.3 6.6 %copy-start.36 = (bf16[384]{0:T(512)(128)(2,1)S(1)}, bf16[384]{0:T(512)(128)(2,1)}, u32[]{:S(2)}) copy-start(bf16[384]{0:T(512)(128)(2,1)} %get-tuple-element.43) | copy-start | bytes 2308
  196.3 6.6 %copy-start.40 = (bf16[384]{0:T(512)(128)(2,1)S(1)}, bf16[384]{0:T(512)(128)(2,1)}, u32[]{:S(2)}) copy-start(bf16[384]{0:T(512)(128)(2,1)} %get-tuple-element.30) | copy-start | bytes 2308
  196.3 6.6 %copy-start.39 = (bf16[384]{0:T(512)(128)(2,1)S(1)}, bf16[384]{0:T(512)(128)(2,1)}, u32[]{:S(2)}) copy-start(bf16[384]{0:T(512)(128)(2,1)} %get-tuple-element.36) | copy-start | bytes 2308
  196.3 6.6 %copy-start.35 = (bf16[1,384]{1,0:T(2,128)(2,1)S(1)}, bf16[1,384]{1,0:T(2,128)(2,1)}, u32[]{:S(2)}) copy-start(bf16[1,384]{1,0:T(2,128)(2,1)} %stack.43) | copy-start | bytes 2308
  201.2 6.7 %copy-start.37 = (bf16[1536]{0:T(1024)(128)(2,1)S(1)}, bf16[1536]{0:T(1024)(128)(2,1)}, u32[]{:S(2)}) copy-start(bf16[1536]{0:T(1024)(128)(2,1)} %get-tuple-element.69) | copy-start | bytes 9220
  203.0 3.1 copy-start.6
  206.2 4.6 copy-start.41
  210.7 205.6 %all-reduce.4.cloned.1.call-start = ((), (), s32[]{:S(2)}) async-start(), calls=%async_computation.1 | async-start | bytes 7110656 | tf_op jit(solution)/shard_map/psum | solution.py:206
  212.0 204.3 %copy-start.24 = (f32[55552]{0:T(1024)S(1)}, f32[55552]{0:T(1024)}, u32[]{:S(2)}) copy-start(f32[55552]{0:T(1024)} %param.8) | copy-start | bytes 666628
  212.0 204.3 %copy-start.25 = (f32[55552]{0:T(1024)S(1)}, f32[55552]{0:T(1024)}, u32[]{:S(2)}) copy-start(f32[55552]{0:T(1024)} %param.9) | copy-start | bytes 666628
  309.1 142.6 %copy-start.38 = (f32[384]{0:T(512)S(1)}, f32[384]{0:T(512)}, u32[]{:S(2)}) copy-start(f32[384]{0:T(512)} %get-tuple-element.49) | copy-start | bytes 4612
  418.6 4.1 collective-permute-start
  422.6 8.1 %collective-permute-start.1 = (f32[55552]{0:T(1024)S(1)}, f32[55552]{0:T(1024)S(1)}, u32[]{:S(2)}, u32[]{:S(2)}) collective-permute-start(f32[55552]{0:T(1024)S(1)} %collective-permute-done), channel_id=1, source_target_pairs={{0,15},{1,0},{2,1},{3,2},{4,3},{5,4},{6,5},{7,6},{8,7},{9,8},{10,9... | collective-permute-start | bytes 666632 | tf_op jit(solution)/shard_map/ppermute | solution.py:24
  430.7 25.2 %copy-start.16 = (f32[55552]{0:T(1024)}, f32[55552]{0:T(1024)S(1)}, u32[]{:S(2)}) copy-start(f32[55552]{0:T(1024)S(1)} %collective-permute-done.1) | copy-start | bytes 666628
  430.7 8.1 %collective-permute-start.2 = (f32[55552]{0:T(1024)S(1)}, f32[55552]{0:T(1024)S(1)}, u32[]{:S(2)}, u32[]{:S(2)}) collective-permute-start(f32[55552]{0:T(1024)S(1)} %collective-permute-done.1), channel_id=1, source_target_pairs={{0,15},{1,0},{2,1},{3,2},{4,3},{5,4},{6,5},{7,6},{8,7},{9,8},{10,9... | collective-permute-start | bytes 666632 | tf_op jit(solution)/shard_map/ppermute | solution.py:24
  438.8 17.1 %copy-start.18 = (f32[55552]{0:T(1024)}, f32[55552]{0:T(1024)S(1)}, u32[]{:S(2)}) copy-start(f32[55552]{0:T(1024)S(1)} %collective-permute-done.2) | copy-start | bytes 666628
  438.8 8.1 %collective-permute-start.3 = (f32[55552]{0:T(1024)S(1)}, f32[55552]{0:T(1024)}, u32[]{:S(2)}, u32[]{:S(2)}) collective-permute-start(f32[55552]{0:T(1024)S(1)} %collective-permute-done.2), channel_id=1, source_target_pairs={{0,15},{1,0},{2,1},{3,2},{4,3},{5,4},{6,5},{7,6},{8,7},{9,8},{10,9... | collective-permute-start | bytes 666632 | tf_op jit(solution)/shard_map/ppermute | solution.py:24
  446.9 11.3 %collective-permute-start.4 = (f32[55552]{0:T(1024)}, f32[55552]{0:T(1024)}, u32[]{:S(2)}, u32[]{:S(2)}) collective-permute-start(f32[55552]{0:T(1024)} %collective-permute-done.3), channel_id=1, source_target_pairs={{0,15},{1,0},{2,1},{3,2},{4,3},{5,4},{6,5},{7,6},{8,7},{9,8},{10,9... | collective-permute-start | bytes 666632 | tf_op jit(solution)/shard_map/ppermute | solution.py:24
  458.2 5.7 collective-permute-start.5
  463.9 12.7 %copy-start.20 = (f32[55552]{0:T(1024)}, f32[55552]{0:T(1024)S(1)}, u32[]{:S(2)}) copy-start(f32[55552]{0:T(1024)S(1)} %collective-permute-done.5) | copy-start | bytes 666628
  463.9 8.0 %collective-permute-start.6 = (f32[55552]{0:T(1024)S(1)}, f32[55552]{0:T(1024)}, u32[]{:S(2)}, u32[]{:S(2)}) collective-permute-start(f32[55552]{0:T(1024)S(1)} %collective-permute-done.5), channel_id=1, source_target_pairs={{0,15},{1,0},{2,1},{3,2},{4,3},{5,4},{6,5},{7,6},{8,7},{9,8},{10,9... | collective-permute-start | bytes 666632 | tf_op jit(solution)/shard_map/ppermute | solution.py:24
  471.9 8.5 %collective-permute-start.7 = (f32[55552]{0:T(1024)}, f32[55552]{0:T(1024)}, u32[]{:S(2)}, u32[]{:S(2)}) collective-permute-start(f32[55552]{0:T(1024)} %collective-permute-done.6), channel_id=1, source_target_pairs={{0,15},{1,0},{2,1},{3,2},{4,3},{5,4},{6,5},{7,6},{8,7},{9,8},{10,9... | collective-permute-start | bytes 666632 | tf_op jit(solution)/shard_map/ppermute | solution.py:24
  476.6 10.1 %copy-start.17 = (f32[55552]{0:T(1024)S(1)}, f32[55552]{0:T(1024)}, u32[]{:S(2)}) copy-start(f32[55552]{0:T(1024)} %copy-done.16) | copy-start | bytes 666628
  476.6 16.7 %copy-start.19 = (f32[55552]{0:T(1024)S(1)}, f32[55552]{0:T(1024)}, u32[]{:S(2)}) copy-start(f32[55552]{0:T(1024)} %copy-done.18) | copy-start | bytes 666628
  478.8 24.3 %copy-start.21 = (f32[55552]{0:T(1024)S(1)}, f32[55552]{0:T(1024)}, u32[]{:S(2)}) copy-start(f32[55552]{0:T(1024)} %copy-done.20) | copy-start | bytes 666628
  480.4 8.4 %collective-permute-start.8 = (f32[55552]{0:T(1024)}, f32[55552]{0:T(1024)S(1)}, u32[]{:S(2)}, u32[]{:S(2)}) collective-permute-start(f32[55552]{0:T(1024)} %collective-permute-done.7), channel_id=1, source_target_pairs={{0,15},{1,0},{2,1},{3,2},{4,3},{5,4},{6,5},{7,6},{8,7},{9,8},{10,9... | collective-permute-start | bytes 666632 | tf_op jit(solution)/shard_map/ppermute | solution.py:24
  488.8 8.0 %collective-permute-start.9 = (f32[55552]{0:T(1024)S(1)}, f32[55552]{0:T(1024)S(1)}, u32[]{:S(2)}, u32[]{:S(2)}) collective-permute-start(f32[55552]{0:T(1024)S(1)} %collective-permute-done.8), channel_id=1, source_target_pairs={{0,15},{1,0},{2,1},{3,2},{4,3},{5,4},{6,5},{7,6},{8,7},{9,8},{10,9... | collective-permute-start | bytes 666632 | tf_op jit(solution)/shard_map/ppermute | solution.py:24
  496.8 8.1 %collective-permute-start.10 = (f32[55552]{0:T(1024)S(1)}, f32[55552]{0:T(1024)S(1)}, u32[]{:S(2)}, u32[]{:S(2)}) collective-permute-start(f32[55552]{0:T(1024)S(1)} %collective-permute-done.9), channel_id=1, source_target_pairs={{0,15},{1,0},{2,1},{3,2},{4,3},{5,4},{6,5},{7,6},{8,7},{9,8},{10,9... | collective-permute-start | bytes 666632 | tf_op jit(solution)/shard_map/ppermute | solution.py:24
  504.9 8.1 %collective-permute-start.11 = (f32[55552]{0:T(1024)S(1)}, f32[55552]{0:T(1024)S(1)}, u32[]{:S(2)}, u32[]{:S(2)}) collective-permute-start(f32[55552]{0:T(1024)S(1)} %collective-permute-done.10), channel_id=1, source_target_pairs={{0,15},{1,0},{2,1},{3,2},{4,3},{5,4},{6,5},{7,6},{8,7},{9,8},{10,9... | collective-permute-start | bytes 666632 | tf_op jit(solution)/shard_map/ppermute | solution.py:24
  513.0 8.1 %collective-permute-start.12 = (f32[55552]{0:T(1024)S(1)}, f32[55552]{0:T(1024)S(1)}, u32[]{:S(2)}, u32[]{:S(2)}) collective-permute-start(f32[55552]{0:T(1024)S(1)} %collective-permute-done.11), channel_id=1, source_target_pairs={{0,15},{1,0},{2,1},{3,2},{4,3},{5,4},{6,5},{7,6},{8,7},{9,8},{10,9... | collective-permute-start | bytes 666632 | tf_op jit(solution)/shard_map/ppermute | solution.py:24
  521.1 8.1 %collective-permute-start.13 = (f32[55552]{0:T(1024)S(1)}, f32[55552]{0:T(1024)S(1)}, u32[]{:S(2)}, u32[]{:S(2)}) collective-permute-start(f32[55552]{0:T(1024)S(1)} %collective-permute-done.12), channel_id=1, source_target_pairs={{0,15},{1,0},{2,1},{3,2},{4,3},{5,4},{6,5},{7,6},{8,7},{9,8},{10,9... | collective-permute-start | bytes 666632 | tf_op jit(solution)/shard_map/ppermute | solution.py:24
  529.2 8.1 %collective-permute-start.14 = (f32[55552]{0:T(1024)S(1)}, f32[55552]{0:T(1024)S(1)}, u32[]{:S(2)}, u32[]{:S(2)}) collective-permute-start(f32[55552]{0:T(1024)S(1)} %collective-permute-done.13), channel_id=1, source_target_pairs={{0,15},{1,0},{2,1},{3,2},{4,3},{5,4},{6,5},{7,6},{8,7},{9,8},{10,9... | collective-permute-start | bytes 666632 | tf_op jit(solution)/shard_map/ppermute | solution.py:24
Sparse Core Ops, SparseCore 0:
  10.8 52.2 all-gather.1
  210.8 94.7 all-reduce.5
  309.8 106.4 all-reduce.3
